TPU v7x, 512 devices: a whole 4x4x16 slice. The times are simulated.
512 devices in a mesh: section: 2 (over x_hi), expert: 32 (over z, core), tensor: 8 (over x_lo, y).
Axes of the slice: x: 4 (x_hi: 2, x_lo: 2; x = x_hi * 2 + x_lo), y: 4, z: 16, core: 2. Of those that a mesh axis runs over, the one named last changes fastest.
Arguments:
- tokens: bfloat16 [8192, 2880], P(('section', 'expert'), 'tensor'), may hold values from -6 to 6
- expert_ids: int32 [8192, 4], P(('section', 'expert')), may hold values from 0 to 63, as said below
- gates: float32 [8192, 4], P(('section', 'expert')), may hold values from 0.05 to 0.5
- remap: int32 [64], replicated, may hold values from 0 to 63, as said below
- gate_up: bfloat16 [64, 2, 1440, 2880], P(('section', 'expert'), None, 'tensor'), may hold values from -0.109375 to 0.109375
- down: bfloat16 [64, 1440, 2880], P(('section', 'expert'), None, 'tensor'), may hold values from -0.15625 to 0.15625
- norm_gain: float32 [2880], replicated, may hold values from 0.25 to 1.75
- w_query: bfloat16 [2880, 2048], P(('section', 'expert'), 'tensor'), may hold values from -2 to 2
- w_key: bfloat16 [2880, 512], P(('section', 'expert'), 'tensor'), may hold values from -2 to 2
- w_value: bfloat16 [2880, 512], P(('section', 'expert'), 'tensor'), may hold values from -0.109375 to 0.109375
- w_out: bfloat16 [2048, 2880], P('tensor', ('section', 'expert')), may hold values from -0.125 to 0.125
Outputs:
- stream: bfloat16 [8192, 2880], P(('section', 'expert'), 'tensor')
- attended: bfloat16 [8192, 2880], P(('section', 'expert'), 'tensor')
Inputs may be any that keep to these rules, and one draw needn't show every extreme that they name: `remap`: every expert maps to itself, except the 4 experts of one aligned group of 4 (a failed host), which map to 4 different surviving experts. `expert_ids`: each row names 4 different experts, and their images under remap differ too. In every aligned block of 128 rows, after the remap, 4 surviving experts receive exactly 16 picks each, every other surviving expert exactly 8, the experts of the failed host none.
All inputs are finite; a program needn't handle non-finite values.
Results may differ from a plain program's by a relative error of at most 0.033.
Values may be sent and summed in bfloat16 or wider, within the bound.
No kernel may reach another device: no remote copies, remote signals or barrier semaphores. Data moves between devices by JAX's collectives and lax.ppermute only.
A program may use at most 64 MiB of HBM per device.

v0:
```python
import math
import jax
import jax.numpy as jnp
from jax import lax
from jax.sharding import PartitionSpec as P

D = 2880
HD = 64
epsilon = 1e-05


def rotate_pairs(values, positions):
    half_size = values.shape[-1] // 2
    freq = jnp.exp(
        -math.log(150000.0) * jnp.arange(half_size, dtype=jnp.float32) * 2.0 / values.shape[-1]
    )
    angle = positions.astype(jnp.float32)[:, None] * freq[None, :]
    cosine = jnp.cos(angle)[:, None, :]
    sine = jnp.sin(angle)[:, None, :]
    first_half = values[..., :half_size]
    second_half = values[..., half_size:]
    return jnp.concatenate(
        [first_half * cosine - second_half * sine, second_half * cosine + first_half * sine],
        axis=-1,
    )


def on_device(
    tokens, expert_ids, gates, remap, gate_up, down, norm_gain, w_query, w_key, w_value, w_out
):
    token_rows = tokens.shape[0]
    slice_width = tokens.shape[1]
    topk_count = expert_ids.shape[1]
    groups = lax.axis_size(("section", "expert"))
    capacity = 2 * token_rows * topk_count // groups
    physical = remap[expert_ids].reshape(-1)
    pick_count = physical.shape[0]
    pick_token = jnp.arange(pick_count, dtype=jnp.int32) // topk_count
    one_hot = (physical[:, None] == jnp.arange(groups, dtype=jnp.int32)[None, :]).astype(jnp.int32)
    pick_rank = jnp.sum((jnp.cumsum(one_hot, axis=0) - 1) * one_hot, axis=1)
    slot_index = physical * capacity + pick_rank
    slot_hits = slot_index[:, None] == jnp.arange(groups * capacity, dtype=jnp.int32)[None, :]
    slot_token = jnp.sum(jnp.where(slot_hits, pick_token[:, None], 0), axis=0)
    slot_used = jnp.any(slot_hits, axis=0)
    local_hidden = gate_up.shape[2]
    local_expert = gate_up[0].reshape(2 * local_hidden, gate_up.shape[3])
    whole_tokens = lax.all_gather(tokens, "tensor", axis=1, tiled=True)
    outgoing = jnp.where(
        slot_used[:, None], whole_tokens[slot_token], jnp.zeros((), jnp.bfloat16)
    ).reshape(groups, capacity, -1)
    arrived = lax.all_to_all(
        outgoing, ("section", "expert"), split_axis=0, concat_axis=0, tiled=True
    )
    source_count = arrived.shape[0]
    rows_in = arrived.reshape(-1, arrived.shape[2])
    projected = lax.dot_general(
        rows_in, local_expert, (((1,), (1,)), ((), ())), preferred_element_type=jnp.float32
    )
    hidden = (jax.nn.silu(projected[:, :local_hidden]) * projected[:, local_hidden:]).astype(
        jnp.bfloat16
    )
    all_hidden = lax.all_gather(hidden, "tensor", axis=1, tiled=True)
    result = jnp.dot(all_hidden, down[0], preferred_element_type=jnp.float32).astype(jnp.bfloat16)
    result = result.reshape(source_count, -1, result.shape[1])
    returned = lax.all_to_all(
        result, ("section", "expert"), split_axis=0, concat_axis=0, tiled=True
    )
    back_rows = returned.reshape(groups * capacity, -1)[slot_index]
    mixture = jnp.sum(
        back_rows.astype(jnp.float32).reshape(token_rows, topk_count, -1) * gates[:, :, None],
        axis=1,
    )
    stream = (tokens.astype(jnp.float32) + mixture).astype(jnp.bfloat16)
    stream_wide = stream.astype(jnp.float32)
    squares = lax.psum(jnp.sum(stream_wide * stream_wide, axis=1), "tensor")
    gain_part = lax.dynamic_slice_in_dim(
        norm_gain, lax.axis_index("tensor") * slice_width, slice_width
    )
    normed_part = (
        stream_wide * lax.rsqrt(squares / D + epsilon)[:, None] * gain_part[None, :]
    ).astype(jnp.bfloat16)
    normed = lax.all_gather(normed_part, "tensor", axis=1, tiled=True)
    query_width = w_query.shape[1]
    kv_width = w_key.shape[1]
    pieces = (
        lax.all_gather(w_query, ("section", "expert"), axis=0, tiled=True),
        lax.all_gather(w_key, ("section", "expert"), axis=0, tiled=True),
        lax.all_gather(w_value, ("section", "expert"), axis=0, tiled=True),
    )
    query_raw, key_raw, value_raw = tuple(
        (jnp.dot(normed, piece, preferred_element_type=jnp.float32) for piece in pieces)
    )
    positions = lax.axis_index("expert") * token_rows + jnp.arange(token_rows, dtype=jnp.int32)
    query_heads = query_width // HD
    kv_heads = kv_width // HD
    group_size = query_heads // kv_heads
    queries = rotate_pairs(query_raw.reshape(token_rows, query_heads, HD), positions).astype(
        jnp.bfloat16
    )
    keys = (
        rotate_pairs(key_raw.reshape(token_rows, kv_heads, HD), positions)
        .astype(jnp.bfloat16)
        .reshape(token_rows, kv_width)
    )
    values = value_raw.astype(jnp.bfloat16)
    grouped = queries.reshape(token_rows, kv_heads, group_size, HD)
    pieces = (
        lax.all_gather(keys, "expert", axis=0, tiled=True),
        lax.all_gather(values, "expert", axis=0, tiled=True),
    )
    running_max = jnp.full((kv_heads, group_size, token_rows), -1e30, jnp.float32)
    key_piece = pieces[0].reshape(-1, kv_heads, HD)
    value_piece = pieces[1].reshape(-1, kv_heads, HD)
    key_count = key_piece.shape[0]
    scores = jnp.einsum(
        "tkgd,nkd->kgtn", grouped, key_piece, preferred_element_type=jnp.float32
    ) / math.sqrt(HD)
    key_positions = jnp.arange(key_count, dtype=jnp.int32)
    allowed = key_positions[None, :] <= positions[:, None]
    scores = jnp.where(allowed, scores, -1e30)
    new_max = jnp.maximum(running_max, jnp.max(scores, axis=-1))
    weights = jnp.where(allowed, jnp.exp(scores - new_max[..., None]), 0.0)
    new_sum = jnp.sum(weights, axis=-1)
    weights_low = weights.astype(jnp.bfloat16)
    new_acc = jnp.einsum(
        "kgtn,nkd->kgtd", weights_low, value_piece, preferred_element_type=jnp.float32
    )
    heads = (
        (new_acc / new_sum[..., None])
        .transpose(2, 0, 1, 3)
        .reshape(token_rows, query_width)
        .astype(jnp.bfloat16)
    )
    partial_out = jnp.dot(
        heads,
        lax.all_gather(w_out, ("section", "expert"), axis=1, tiled=True),
        preferred_element_type=jnp.float32,
    )
    attended = lax.psum_scatter(
        partial_out.astype(jnp.bfloat16), "tensor", scatter_dimension=1, tiled=True
    )
    return (stream, attended)


def solution(mesh):
    return jax.shard_map(
        on_device,
        mesh=mesh,
        in_specs=(
            P(("section", "expert"), "tensor"),
            P(("section", "expert"), None),
            P(("section", "expert"), None),
            P(),
            P(("section", "expert"), None, "tensor", None),
            P(("section", "expert"), None, "tensor"),
            P(),
            P(("section", "expert"), "tensor"),
            P(("section", "expert"), "tensor"),
            P(("section", "expert"), "tensor"),
            P("tensor", ("section", "expert")),
        ),
        out_specs=(P(("section", "expert"), "tensor"), P(("section", "expert"), "tensor")),
        check_vma=False,
    )
```

profile of v0, /device:TPU:32, one launch (start us, length us, event | category | flops | bytes accessed | tf_op | source)
XLA Modules:
  0.0 853.0 jit_solution(9896610226944616474)
XLA Ops:
  7.2 0.8 compare_select_fusion.2
  8.0 0.1 copy.55
  8.1 0.1 reshape.284
  8.2 3.3 gather_fusion
  11.6 1.2 reduce-window.6
  12.8 0.2 slice_reduce_fusion
  13.1 0.1 fusion.24
  13.2 0.4 fusion.7
  13.6 0.3 select_reduce_fusion
  13.9 30.1 %all_gather.27 = bf16[128,2880]{0,1:T(8,128)(2,1)S(1)} all-gather(bf16[128,360]{0,1:T(8,128)(2,1)S(1)} %copy-done.5), channel_id=1, replica_groups=mesh['section'=2,'expert'=32,'tensor'=8] {'tensor'}, dimensions={1}, use_global_device_ids=true | all-gather | bytes 829440 | tf_op jit(solution)/shard_map/all_gather | solution.py:47
  44.0 0.4 copy.57
  44.4 0.1 broadcast_in_dim.43
  44.5 6.6 gather_fusion.1
  51.1 5.9 broadcast_select_fusion
  57.0 18.1 %all-to-all-start = ((bf16[64,16,2880]{2,1,0:T(8,128)(2,1)}), bf16[64,16,2880]{2,1,0:T(8,128)(2,1)}, u32[]{:S(2)}, u32[]{:S(2)}) async-start(bf16[64,16,2880]{2,1,0:T(8,128)(2,1)} %broadcast_select_fusion), calls=%async_computation | async-start | bytes 12058624 | tf_op jit(solution)/shard_map/all_to_all | solution.py:51
  75.1 0.0 all-gather.9.cloned.1.call-start
  75.1 1.8 copy.58
  76.9 2.3 reshape_squeeze.3
  79.3 257.8 %all-to-all-done = bf16[64,16,2880]{2,1,0:T(8,128)(2,1)} async-done(((bf16[64,16,2880]{2,1,0:T(8,128)(2,1)}), bf16[64,16,2880]{2,1,0:T(8,128)(2,1)}, u32[]{:S(2)}, u32[]{:S(2)}) %all-to-all-start) | async-done | bytes 5898272 | tf_op jit(solution)/shard_map/all_to_all | solution.py:51
  337.1 5.8 fusion.47
  343.0 1.0 fusion.19
  343.9 0.0 all-gather.9.cloned.1.call-update
  344.0 0.0 all-gather.11.cloned.1.call-start
  344.0 0.7 all-gather.11.cloned.1.call-update
  344.7 0.0 all-gather.13.cloned.1.call-start
  344.8 0.7 all-gather.13.cloned.1.call-update
  345.5 47.8 %all-gather.9.cloned.1.call-done = bf16[8,180,1024]{2,1,0:T(8,128)(2,1)} async-done(((bf16[1,180,1024]{2,1,0:T(8,128)(2,1)}), bf16[8,180,1024]{2,1,0:T(8,128)(2,1)}) %all-gather.9.cloned.1.call-update) | async-done | bytes 2949136 | tf_op jit(solution)/shard_map/all_gather | solution.py:62
  393.2 4.3 reshape.315
  397.6 3.2 convolution_convert_fusion.1
  400.8 1.2 copy.59
  402.0 15.3 %all-to-all-start.1 = ((bf16[64,16,360]{2,1,0:T(8,128)(2,1)}), bf16[64,16,360]{2,1,0:T(8,128)(2,1)S(1)}, u32[]{:S(2)}, u32[]{:S(2)}) async-start(bf16[64,16,360]{2,1,0:T(8,128)(2,1)} %bitcast.9), calls=%async_computation.1 | async-start | bytes 1572864 | tf_op jit(solution)/shard_map/all_to_all | solution.py:65
  417.3 0.0 reduce-scatter.5.cloned.1.call-start
  417.4 0.1 copy.54
  417.5 0.1 copy.60
  417.6 104.8 %all-gather.1 = bf16[64,45,64]{2,1,0:T(8,128)(2,1)S(1)} all-gather(bf16[1,45,64]{2,1,0:T(8,128)(2,1)S(1)} %bitcast.105), channel_id=1, replica_groups=mesh['section'=2,'expert'=32,'tensor'=8] {'section','expert'}, dimensions={0}, use_global_device_ids=true | all-gather | bytes 374400 | tf_op jit(solution)/shard_map/all_gather | solution.py:87
  522.5 1.1 reshape.326
  523.6 76.3 %all-gather.3 = bf16[64,45,64]{2,1,0:T(8,128)(2,1)S(1)} all-gather(bf16[1,45,64]{2,1,0:T(8,128)(2,1)S(1)} %bitcast.106), channel_id=1, replica_groups=mesh['section'=2,'expert'=32,'tensor'=8] {'section','expert'}, dimensions={0}, use_global_device_ids=true | all-gather | bytes 374400 | tf_op jit(solution)/shard_map/all_gather | solution.py:88
  600.0 1.1 reshape.327
  601.1 0.8 dynamic_slice.3
  601.9 0.8 multiply_cosine_fusion
  602.7 1.1 iota_compare_fusion
  603.8 3.4 reshape.319
  607.2 74.6 %all-gather.13.cloned.1.call-done = bf16[64,45,256]{2,1,0:T(8,128)(2,1)} async-done(((bf16[1,45,256]{2,1,0:T(8,128)(2,1)}), bf16[64,45,256]{2,1,0:T(8,128)(2,1)}) %all-gather.13.cloned.1.call-update) | async-done | bytes 1474576 | tf_op jit(solution)/shard_map/all_gather | solution.py:136
  681.8 2.4 reshape.323
  684.2 2.6 gather_fusion.2
  686.8 1.2 reshape.281
  688.0 0.5 multiply_reduce_fusion
  688.6 0.1 fusion.20
  688.7 18.8 %psum.7 = f32[128]{0:T(128)S(1)} all-reduce(f32[128]{0:T(128)S(1)} %get-tuple-element.8), channel_id=1, replica_groups=mesh['section'=2,'expert'=32,'tensor'=8] {'tensor'}, use_global_device_ids=true, to_apply=%region_7.8 | all-reduce | flops 128 | bytes 1024 | tf_op jit(solution)/shard_map/psum | solution.py:75
  707.5 0.1 fusion.22
  707.6 0.1 copy.61
  707.8 29.7 %all_gather.29 = bf16[128,2880]{0,1:T(8,128)(2,1)S(1)} all-gather(bf16[128,360]{0,1:T(8,128)(2,1)S(1)} %copy.61), channel_id=1, replica_groups=mesh['section'=2,'expert'=32,'tensor'=8] {'tensor'}, dimensions={1}, use_global_device_ids=true | all-gather | bytes 829440 | tf_op jit(solution)/shard_map/all_gather | solution.py:82
  737.5 1.5 convolution_bitcast_fusion
  739.0 0.7 fusion.38
  739.8 28.8 %all_gather.31 = bf16[4096,64]{0,1:T(8,128)(2,1)S(1)} all-gather(bf16[128,64]{0,1:T(8,128)(2,1)S(1)} %pad_maximum_fusion), channel_id=1, replica_groups=mesh['section'=2,'expert'=32,'tensor'=8] {'expert'}, dimensions={0}, use_global_device_ids=true | all-gather | bytes 540672 | tf_op jit(solution)/shard_map/all_gather | solution.py:108
  768.6 0.7 fusion.48
  769.4 1.3 fusion
  770.7 0.4 convolution_convert_fusion.2
  771.1 30.1 %all_gather.34 = bf16[4096,64]{0,1:T(8,128)(2,1)S(1)} all-gather(bf16[128,64]{0,1:T(8,128)(2,1)S(1)} %convolution_convert_fusion.2), channel_id=1, replica_groups=mesh['section'=2,'expert'=32,'tensor'=8] {'expert'}, dimensions={0}, use_global_device_ids=true | all-gather | bytes 540672 | tf_op jit(solution)/shard_map/all_gather | solution.py:109
  801.2 2.1 fusion.1
  803.2 1.8 fusion.12
  805.1 1.4 convolution_convert_fusion
  806.5 0.8 copy.66
  807.3 39.2 %reduce-scatter.5.cloned.1.call-done = bf16[128,360]{0,1:T(8,128)(2,1)} async-done(((bf16[128,2880]{0,1:T(8,128)(2,1)}), bf16[128,360]{0,1:T(8,128)(2,1)}) %reduce-scatter.5.cloned.1.call-update) | async-done | bytes 92176
  (45 shorter events, 0.2 us)
Async XLA Ops:
  7.2 390.4 %copy-start = (bf16[1,1440,360]{2,1,0:T(8,128)(2,1)S(1)}, bf16[1,1440,360]{2,1,0:T(8,128)(2,1)}, u32[]{:S(2)}) copy-start(bf16[1,1440,360]{2,1,0:T(8,128)(2,1)} %param.16) | copy-start | bytes 3110404
  7.2 1.0 copy-start.1
  8.2 5.7 copy-start.5
  57.0 280.1 %all-to-all-start = ((bf16[64,16,2880]{2,1,0:T(8,128)(2,1)}), bf16[64,16,2880]{2,1,0:T(8,128)(2,1)}, u32[]{:S(2)}, u32[]{:S(2)}) async-start(bf16[64,16,2880]{2,1,0:T(8,128)(2,1)} %broadcast_select_fusion), calls=%async_computation | async-start | bytes 12058624 | tf_op jit(solution)/shard_map/all_to_all | solution.py:51
  75.1 318.2 %all-gather.9.cloned.1.call-start = ((), (), s32[]{:S(2)}) async-start(), calls=%async_computation.3 | async-start | bytes 3391488 | tf_op jit(solution)/shard_map/all_gather | solution.py:62
  344.0 259.9 %all-gather.11.cloned.1.call-start = ((), (), s32[]{:S(2)}) async-start(), calls=%async_computation.4 | async-start | bytes 1597440 | tf_op jit(solution)/shard_map/all_gather | solution.py:86
  344.7 337.1 %all-gather.13.cloned.1.call-start = ((), (), s32[]{:S(2)}) async-start(), calls=%async_computation.5 | async-start | bytes 1597440 | tf_op jit(solution)/shard_map/all_gather | solution.py:136
  400.8 16.7 %copy-start.12 = (f32[128,4]{0,1:T(4,128)S(1)}, f32[128,4]{0,1:T(4,128)}, u32[]{:S(2)}) copy-start(f32[128,4]{0,1:T(4,128)} %param.13) | copy-start | bytes 6148
  400.8 16.8 %copy-start.7 = (bf16[45,64]{1,0:T(8,128)(2,1)S(1)}, bf16[45,64]{1,0:T(8,128)(2,1)}, u32[]{:S(2)}) copy-start(bf16[45,64]{1,0:T(8,128)(2,1)} %param.19) | copy-start | bytes 17284
  400.8 122.8 %copy-start.8 = (bf16[45,64]{1,0:T(8,128)(2,1)S(1)}, bf16[45,64]{1,0:T(8,128)(2,1)}, u32[]{:S(2)}) copy-start(bf16[45,64]{1,0:T(8,128)(2,1)} %param.20) | copy-start | bytes 17284
  402.0 282.2 %all-to-all-start.1 = ((bf16[64,16,360]{2,1,0:T(8,128)(2,1)}), bf16[64,16,360]{2,1,0:T(8,128)(2,1)S(1)}, u32[]{:S(2)}, u32[]{:S(2)}) async-start(bf16[64,16,360]{2,1,0:T(8,128)(2,1)} %bitcast.9), calls=%async_computation.1 | async-start | bytes 1572864 | tf_op jit(solution)/shard_map/all_to_all | solution.py:65
  417.3 429.2 %reduce-scatter.5.cloned.1.call-start = ((), (), s32[]{:S(2)}) async-start(), calls=%async_computation.6 | async-start | bytes 829440
  601.9 5.4 copy-start.9
  601.9 5.3 copy-start.11
  686.8 52.2 %copy-start.10 = (f32[32]{0:T(128)S(1)}, f32[32]{0:T(128)}, u32[]{:S(2)}) copy-start(f32[32]{0:T(128)} %copy-done.9) | copy-start | bytes 388
  688.6 80.8 %copy-start.6 = (f32[128,32]{0,1:T(8,128)S(1)}, f32[128,32]{0,1:T(8,128)}, u32[]{:S(2)}) copy-start(f32[128,32]{0,1:T(8,128)} %get-tuple-element.15) | copy-start | bytes 49156
  688.7 80.7 %copy-start.4 = (pred[128,4096]{0,1:T(8,128)(4,1)S(1)}, pred[128,4096]{0,1:T(8,128)(4,1)}, u32[]{:S(2)}) copy-start(pred[128,4096]{0,1:T(8,128)(4,1)} %iota_compare_fusion) | copy-start | bytes 1572868
  707.8 60.9 %copy-start.2 = (bf16[2880,256]{1,0:T(8,128)(2,1)S(1)}, bf16[2880,256]{1,0:T(8,128)(2,1)}, u32[]{:S(2)}) copy-start(bf16[2880,256]{1,0:T(8,128)(2,1)} %reshape.319) | copy-start | bytes 4423684
  769.4 1.3 copy-start.3
Sparse Core Ops, SparseCore 0:
  344.1 49.0 all-gather.8
  396.5 145.0 all-gather.10
  544.9 136.8 all-gather.12
  806.6 39.8 reduce-scatter.4
where the time goes:
time: 854 us; the launch traced here: 853 us
  waiting for transfers between devices  421 us (49%)
  blocking collectives  319 us (37%)
  local copies, waits for them, and re-layouts  34.3 us (4%)
  starting transfers between devices  33.6 us (4%)
  matrix products  16.1 us (2%)
  other arithmetic  15.2 us (2%)
  between operations  14.2 us (2%)
    all_to_all x1, waiting for transfers between devices, on_device(): lax.all_to_all(outgoing, ('section', 'expert'), split_axis=0, concat_axis...  258 us
    all_gather x1, blocking collectives, on_device(): lax.all_gather(w_key, ('section', 'expert'), axis=0, tiled=True)  105 us
    all_gather x1, blocking collectives, on_device(): lax.all_gather(w_value, ('section', 'expert'), axis=0, tiled=True)  76.3 us
    all_gather x1, waiting for transfers between devices, on_device(): lax.all_gather(w_out, ('section', 'expert'), axis=1, tiled=True)  74.6 us
    all_gather x1, waiting for transfers between devices, on_device(): all_hidden = lax.all_gather(hidden, 'tensor', axis=1, tiled=True)  47.8 us
    unnamed x5, waiting for transfers between devices  40.6 us
    all_gather x1, blocking collectives, on_device(): whole_tokens = lax.all_gather(tokens, 'tensor', axis=1, tiled=True)  30.1 us
    all_gather x1, blocking collectives, on_device(): lax.all_gather(values, 'expert', axis=0, tiled=True)  30.1 us
  transfers between devices with their start and end apart: 6, of which 4 were waited for; matrix products, arithmetic and copies ran while one was open for 3% of the time, Pallas kernels for 0%

commit v1 on v0

--- a/solution.py
+++ b/solution.py
@@ -79,7 +79,9 @@
     normed_part = (
         stream_wide * lax.rsqrt(squares / D + epsilon)[:, None] * gain_part[None, :]
     ).astype(jnp.bfloat16)
-    normed = lax.all_gather(normed_part, "tensor", axis=1, tiled=True)
+    normed = jnp.concatenate(
+        lax.all_to_all(jnp.stack([normed_part] * lax.axis_size("tensor")), "tensor", 0, 0), axis=1
+    )
     query_width = w_query.shape[1]
     kv_width = w_key.shape[1]
     pieces = (

time: 854 us -> 802 us (0.939)
  the two profiles are of different devices: /device:TPU:32 before, /device:TPU:4 now
where the time goes in v1:
time: 802 us; the launch traced here: 801 us
  waiting for transfers between devices  396 us (49%)
  blocking collectives  286 us (36%)
  starting transfers between devices  38.4 us (5%)
  local copies, waits for them, and re-layouts  36.5 us (5%)
  matrix products  16 us (2%)
  between operations  14.1 us (2%)
  other arithmetic  14 us (2%)
    all_to_all x1, waiting for transfers between devices, on_device(): lax.all_to_all(outgoing, ('section', 'expert'), split_axis=0, concat_axis...  263 us
    all_gather x1, blocking collectives, on_device(): lax.all_gather(w_key, ('section', 'expert'), axis=0, tiled=True)  105 us
    all_gather x1, blocking collectives, on_device(): lax.all_gather(w_value, ('section', 'expert'), axis=0, tiled=True)  73.9 us
    all_gather x1, waiting for transfers between devices, on_device(): lax.all_gather(w_out, ('section', 'expert'), axis=1, tiled=True)  46.1 us
    unnamed x5, waiting for transfers between devices  44.2 us
    all_gather x1, waiting for transfers between devices, on_device(): all_hidden = lax.all_gather(hidden, 'tensor', axis=1, tiled=True)  43 us
    all_gather x1, blocking collectives, on_device(): lax.all_gather(keys, 'expert', axis=0, tiled=True)  30.3 us
    all_gather x1, blocking collectives, on_device(): whole_tokens = lax.all_gather(tokens, 'tensor', axis=1, tiled=True)  29.8 us
  transfers between devices with their start and end apart: 7, of which 4 were waited for; matrix products, arithmetic and copies ran while one was open for 4% of the time, Pallas kernels for 0%

profile of v1, /device:TPU:4, one launch (start us, length us, event | category | flops | bytes accessed | tf_op | source)
XLA Modules:
  0.0 801.3 jit_solution(10435351109936303661)
XLA Ops:
  7.2 0.8 compare_select_fusion.2
  8.0 0.1 copy.42
  8.1 0.1 reshape.292
  8.2 3.3 gather_fusion
  11.6 1.2 reduce-window.6
  12.8 0.2 slice_reduce_fusion
  13.1 0.1 fusion.24
  13.2 0.4 fusion.7
  13.6 0.3 select_reduce_fusion
  13.9 29.8 %all_gather.24 = bf16[128,2880]{0,1:T(8,128)(2,1)S(1)} all-gather(bf16[128,360]{0,1:T(8,128)(2,1)S(1)} %copy-done.5), channel_id=1, replica_groups=mesh['section'=2,'expert'=32,'tensor'=8] {'tensor'}, dimensions={1}, use_global_device_ids=true | all-gather | bytes 829440 | tf_op jit(solution)/shard_map/all_gather | solution.py:47
  43.7 0.4 copy.44
  44.1 0.1 broadcast_in_dim.43
  44.2 6.6 gather_fusion.1
  50.8 5.9 broadcast_select_fusion
  56.7 18.9 %all-to-all-start = ((bf16[64,16,2880]{2,1,0:T(8,128)(2,1)}), bf16[64,16,2880]{2,1,0:T(8,128)(2,1)}, u32[]{:S(2)}, u32[]{:S(2)}) async-start(bf16[64,16,2880]{2,1,0:T(8,128)(2,1)} %broadcast_select_fusion), calls=%async_computation | async-start | bytes 12058624 | tf_op jit(solution)/shard_map/all_to_all | solution.py:51
  75.6 0.0 all-gather.9.cloned.1.call-start
  75.6 1.8 copy.45
  77.4 2.3 reshape_squeeze.3
  79.8 262.8 %all-to-all-done = bf16[64,16,2880]{2,1,0:T(8,128)(2,1)} async-done(((bf16[64,16,2880]{2,1,0:T(8,128)(2,1)}), bf16[64,16,2880]{2,1,0:T(8,128)(2,1)}, u32[]{:S(2)}, u32[]{:S(2)}) %all-to-all-start) | async-done | bytes 5898272 | tf_op jit(solution)/shard_map/all_to_all | solution.py:51
  342.6 5.8 fusion.47
  348.4 1.0 fusion.19
  349.5 0.0 all-gather.11.cloned.1.call-start
  349.5 0.7 all-gather.11.cloned.1.call-update
  350.2 43.0 %all-gather.9.cloned.1.call-done = bf16[8,180,1024]{2,1,0:T(8,128)(2,1)} async-done(((bf16[1,180,1024]{2,1,0:T(8,128)(2,1)}), bf16[8,180,1024]{2,1,0:T(8,128)(2,1)}) %all-gather.9.cloned.1.call-update) | async-done | bytes 2949136 | tf_op jit(solution)/shard_map/all_gather | solution.py:62
  393.2 4.3 reshape.323
  397.6 3.2 convolution_convert_fusion.1
  400.8 1.2 copy.46
  402.0 15.8 %all-to-all-start.1 = ((bf16[64,16,360]{2,1,0:T(8,128)(2,1)}), bf16[64,16,360]{2,1,0:T(8,128)(2,1)S(1)}, u32[]{:S(2)}, u32[]{:S(2)}) async-start(bf16[64,16,360]{2,1,0:T(8,128)(2,1)} %bitcast.9), calls=%async_computation.1 | async-start | bytes 1572864 | tf_op jit(solution)/shard_map/all_to_all | solution.py:65
  417.9 0.7 all-gather.13.cloned.1.call-update
  418.6 105.3 %all-gather.1 = bf16[64,45,64]{2,1,0:T(8,128)(2,1)S(1)} all-gather(bf16[1,45,64]{2,1,0:T(8,128)(2,1)S(1)} %bitcast.115), channel_id=1, replica_groups=mesh['section'=2,'expert'=32,'tensor'=8] {'section','expert'}, dimensions={0}, use_global_device_ids=true | all-gather | bytes 374400 | tf_op jit(solution)/shard_map/all_gather | solution.py:89
  523.9 0.1 copy.41
  524.0 0.1 copy.47
  524.1 1.1 reshape.335
  525.3 73.9 %all-gather.3 = bf16[64,45,64]{2,1,0:T(8,128)(2,1)S(1)} all-gather(bf16[1,45,64]{2,1,0:T(8,128)(2,1)S(1)} %bitcast.116), channel_id=1, replica_groups=mesh['section'=2,'expert'=32,'tensor'=8] {'section','expert'}, dimensions={0}, use_global_device_ids=true | all-gather | bytes 374400 | tf_op jit(solution)/shard_map/all_gather | solution.py:90
  599.2 1.1 reshape.336
  600.3 0.8 dynamic_slice.3
  601.2 0.1 multiply_cosine_fusion
  601.3 1.9 gather_fusion.2
  603.3 0.2 reshape.289
  603.5 0.5 multiply_reduce_fusion
  604.0 0.1 fusion.20
  604.1 18.2 %psum.7 = f32[128]{0:T(128)S(1)} all-reduce(f32[128]{0:T(128)S(1)} %get-tuple-element.6), channel_id=1, replica_groups=mesh['section'=2,'expert'=32,'tensor'=8] {'tensor'}, use_global_device_ids=true, to_apply=%region_7.8 | all-reduce | flops 128 | bytes 1024 | tf_op jit(solution)/shard_map/psum | solution.py:75
  622.4 0.1 fusion.22
  622.5 0.1 copy.48
  622.6 1.0 stack.2
  623.6 3.5 all-to-all-start.2
  627.1 0.0 reduce-scatter.5.cloned.1.call-start
  627.2 1.1 iota_compare_fusion
  628.3 3.4 reshape.327
  631.7 1.8 copy.50
  633.6 46.1 %all-gather.13.cloned.1.call-done = bf16[64,45,256]{2,1,0:T(8,128)(2,1)} async-done(((bf16[1,45,256]{2,1,0:T(8,128)(2,1)}), bf16[64,45,256]{2,1,0:T(8,128)(2,1)}) %all-gather.13.cloned.1.call-update) | async-done | bytes 1474576 | tf_op jit(solution)/shard_map/all_gather | solution.py:138
  679.7 3.4 reshape.331
  683.1 1.5 convolution_bitcast_fusion
  684.6 0.1 fusion.38
  684.8 30.3 %all_gather.27 = bf16[4096,64]{0,1:T(8,128)(2,1)S(1)} all-gather(bf16[128,64]{0,1:T(8,128)(2,1)S(1)} %pad_maximum_fusion), channel_id=1, replica_groups=mesh['section'=2,'expert'=32,'tensor'=8] {'expert'}, dimensions={0}, use_global_device_ids=true | all-gather | bytes 540672 | tf_op jit(solution)/shard_map/all_gather | solution.py:110
  715.1 0.6 fusion.48
  715.7 1.3 fusion
  717.0 0.4 convolution_convert_fusion.2
  717.4 28.5 %all_gather.30 = bf16[4096,64]{0,1:T(8,128)(2,1)S(1)} all-gather(bf16[128,64]{0,1:T(8,128)(2,1)S(1)} %convolution_convert_fusion.2), channel_id=1, replica_groups=mesh['section'=2,'expert'=32,'tensor'=8] {'expert'}, dimensions={0}, use_global_device_ids=true | all-gather | bytes 540672 | tf_op jit(solution)/shard_map/all_gather | solution.py:111
  745.9 2.1 fusion.1
  748.0 1.8 fusion.12
  749.8 1.4 convolution_convert_fusion
  751.3 0.8 copy.53
  752.0 42.8 %reduce-scatter.5.cloned.1.call-done = bf16[128,360]{0,1:T(8,128)(2,1)} async-done(((bf16[128,2880]{0,1:T(8,128)(2,1)}), bf16[128,360]{0,1:T(8,128)(2,1)}) %reduce-scatter.5.cloned.1.call-update) | async-done | bytes 92176
  (40 shorter events, 0.3 us)
Async XLA Ops:
  7.2 390.4 %copy-start = (bf16[1,1440,360]{2,1,0:T(8,128)(2,1)S(1)}, bf16[1,1440,360]{2,1,0:T(8,128)(2,1)}, u32[]{:S(2)}) copy-start(bf16[1,1440,360]{2,1,0:T(8,128)(2,1)} %param.16) | copy-start | bytes 3110404
  7.2 1.0 copy-start.1
  8.2 5.7 copy-start.5
  56.7 285.9 %all-to-all-start = ((bf16[64,16,2880]{2,1,0:T(8,128)(2,1)}), bf16[64,16,2880]{2,1,0:T(8,128)(2,1)}, u32[]{:S(2)}, u32[]{:S(2)}) async-start(bf16[64,16,2880]{2,1,0:T(8,128)(2,1)} %broadcast_select_fusion), calls=%async_computation | async-start | bytes 12058624 | tf_op jit(solution)/shard_map/all_to_all | solution.py:51
  75.6 317.7 %all-gather.9.cloned.1.call-start = ((), (), s32[]{:S(2)}) async-start(), calls=%async_computation.4 | async-start | bytes 3391488 | tf_op jit(solution)/shard_map/all_gather | solution.py:62
  349.5 278.9 %all-gather.11.cloned.1.call-start = ((), (), s32[]{:S(2)}) async-start(), calls=%async_computation.5 | async-start | bytes 1597440 | tf_op jit(solution)/shard_map/all_gather | solution.py:88
  400.8 17.8 %copy-start.6 = (bf16[45,64]{1,0:T(8,128)(2,1)S(1)}, bf16[45,64]{1,0:T(8,128)(2,1)}, u32[]{:S(2)}) copy-start(bf16[45,64]{1,0:T(8,128)(2,1)} %param.19) | copy-start | bytes 17284
  400.8 123.2 %copy-start.8 = (f32[128,4]{0,1:T(4,128)S(1)}, f32[128,4]{0,1:T(4,128)}, u32[]{:S(2)}) copy-start(f32[128,4]{0,1:T(4,128)} %param.13) | copy-start | bytes 6148
  400.8 124.4 %copy-start.7 = (bf16[45,64]{1,0:T(8,128)(2,1)S(1)}, bf16[45,64]{1,0:T(8,128)(2,1)}, u32[]{:S(2)}) copy-start(bf16[45,64]{1,0:T(8,128)(2,1)} %param.20) | copy-start | bytes 17284
  402.0 199.3 %all-to-all-start.1 = ((bf16[64,16,360]{2,1,0:T(8,128)(2,1)}), bf16[64,16,360]{2,1,0:T(8,128)(2,1)S(1)}, u32[]{:S(2)}, u32[]{:S(2)}) async-start(bf16[64,16,360]{2,1,0:T(8,128)(2,1)} %bitcast.9), calls=%async_computation.1 | async-start | bytes 1572864 | tf_op jit(solution)/shard_map/all_to_all | solution.py:65
  417.8 261.9 %all-gather.13.cloned.1.call-start = ((), (), s32[]{:S(2)}) async-start(), calls=%async_computation.6 | async-start | bytes 1597440 | tf_op jit(solution)/shard_map/all_gather | solution.py:138
  623.6 59.5 %all-to-all-start.2 = ((bf16[8,128,360]{1,2,0:T(8,128)(2,1)}), bf16[8,128,360]{1,2,0:T(8,128)(2,1)S(1)}, u32[]{:S(2)}, u32[]{:S(2)}) async-start(bf16[8,128,360]{1,2,0:T(8,128)(2,1)} %stack.2), calls=%async_computation.2 | async-start | bytes 1474560 | tf_op jit(solution)/shard_map/all_to_all | solution.py:83
  627.1 167.7 %reduce-scatter.5.cloned.1.call-start = ((), (), s32[]{:S(2)}) async-start(), calls=%async_computation.7 | async-start | bytes 829440
  683.1 32.6 %copy-start.4 = (pred[128,4096]{0,1:T(8,128)(4,1)S(1)}, pred[128,4096]{0,1:T(8,128)(4,1)}, u32[]{:S(2)}) copy-start(pred[128,4096]{0,1:T(8,128)(4,1)} %iota_compare_fusion) | copy-start | bytes 1572868
  715.7 1.3 copy-start.3
  748.0 1.8 copy-start.2
Sparse Core Ops, SparseCore 0:
  349.6 43.6 all-gather.8
  396.5 142.8 all-gather.10
  542.8 136.8 all-gather.12
  751.4 43.3 reduce-scatter.4
